TPU v7x, 32 devices: a whole 2x2x4 slice. The times are simulated.
32 devices in a mesh: dp: 8 (over y, x, core), tensor: 4 (over z).
Axes of the slice: x: 2, y: 2, z: 4, core: 2. Of those that a mesh axis runs over, the one named last changes fastest.
Arguments:
- layer_input: bfloat16 [16, 768, 768], P('dp', 'tensor'), may hold values from -6 to 6
- word_segments: int32 [16, 256], P('dp'), may hold values from 0 to 13, never falling along the last dimension, each value on 1 to 36 neighbouring positions
- image_order: int32 [16, 14], P('dp'), may hold values from 0 to 13, each once within a row
- cross_qkv: bfloat16 [3, 768, 768], P(None, None, 'tensor'), may hold values from -0.21875 to 0.21875
- cross_out: bfloat16 [768, 768], P('tensor'), may hold values from -0.875 to 0.875
- self_qkv: bfloat16 [2, 3, 768, 768], P(None, None, None, 'tensor'), may hold values from -0.21875 to 0.21875
- self_out: bfloat16 [2, 768, 768], P(None, 'tensor'), may hold values from -0.875 to 0.875
- ffn_up: bfloat16 [2, 768, 3072], P(None, None, 'tensor'), may hold values from -0.21875 to 0.21875
- ffn_down: bfloat16 [2, 3072, 768], P(None, 'tensor'), may hold values from -0.109375 to 0.109375
- norm_gains: float32 [5, 768], replicated, may hold values from 0.5 to 1.5
- norm_biases: float32 [5, 768], replicated, may hold values from -3 to 3
- out_grad: bfloat16 [16, 768, 768], P('dp', 'tensor'), may hold values from -6 to 6
Outputs:
- layer_output: bfloat16 [16, 768, 768], P('dp', 'tensor')
- input_grad: float32 [16, 768, 768], P('dp', 'tensor')
- cross_qkv_grad: float32 [3, 768, 768], P(None, None, 'tensor')
- cross_out_grad: float32 [768, 768], P('tensor')
- self_qkv_grad: float32 [2, 3, 768, 768], P(None, None, None, 'tensor')
- self_out_grad: float32 [2, 768, 768], P(None, 'tensor')
- ffn_up_grad: float32 [2, 768, 3072], P(None, None, 'tensor')
- ffn_down_grad: float32 [2, 3072, 768], P(None, 'tensor')
- norm_gains_grad: float32 [5, 768], replicated
- norm_biases_grad: float32 [5, 768], replicated
Inputs may be any that keep to these rules, and one draw needn't show every extreme that they name: `word_segments`: in each row the ids never fall along the word slots, and each of the 14 captions has 1 to 36 slots. `image_order`: each row names every image once.
All inputs are finite; a program needn't handle non-finite values.
Results may differ from a plain program's by a relative error of at most 0.035.
Values may be sent and summed in bfloat16 or wider, within the bound.
A program may use at most 192 MiB of HBM per device.

v0:
```python
import jax
import jax.numpy as jnp
from jax import lax
from jax.sharding import PartitionSpec as P

HEAD_DIM = 64
WORDS = 256
CAPTIONS = 14
BOXES = 36
REGIONS = 504
PADS = 8


NORM_EPSILON = 1e-12


def contract_in(hidden, w_words, w_regions):
    if w_regions is None:
        return jnp.einsum("rsd,dc->rsc", hidden, w_words, preferred_element_type=jnp.float32)
    return jnp.concatenate(
        [
            jnp.einsum(
                "rsd,dc->rsc", hidden[:, :WORDS], w_words, preferred_element_type=jnp.float32
            ),
            jnp.einsum(
                "rsd,dc->rsc", hidden[:, WORDS:], w_regions, preferred_element_type=jnp.float32
            ),
        ],
        axis=1,
    )


def contract_back(grad_b, w_words, w_regions):
    if w_regions is None:
        return jnp.einsum("rsc,dc->rsd", grad_b, w_words, preferred_element_type=jnp.float32)
    return jnp.concatenate(
        [
            jnp.einsum(
                "rsc,dc->rsd", grad_b[:, :WORDS], w_words, preferred_element_type=jnp.float32
            ),
            jnp.einsum(
                "rsc,dc->rsd", grad_b[:, WORDS:], w_regions, preferred_element_type=jnp.float32
            ),
        ],
        axis=1,
    )


def weight_grad(hidden, grad_b, by_modality):
    if not by_modality:
        return jnp.einsum("rsd,rsc->dc", hidden, grad_b, preferred_element_type=jnp.float32)
    return jnp.stack(
        [
            jnp.einsum(
                "rsd,rsc->dc",
                hidden[:, :WORDS],
                grad_b[:, :WORDS],
                preferred_element_type=jnp.float32,
            ),
            jnp.einsum(
                "rsd,rsc->dc",
                hidden[:, WORDS:],
                grad_b[:, WORDS:],
                preferred_element_type=jnp.float32,
            ),
        ],
        axis=0,
    )


def head_split(tensor_b):
    return tensor_b.reshape(
        tensor_b.shape[0], tensor_b.shape[1], tensor_b.shape[2] // HEAD_DIM, HEAD_DIM
    )


def masked_scores(query_heads, key_heads, allowed):
    raw_scores = jnp.einsum(
        "rqhd,rkhd->rhqk", query_heads, key_heads, preferred_element_type=jnp.float32
    ) * HEAD_DIM ** (-0.5)
    return jnp.where(allowed[:, None], raw_scores, -1e30)


def region_matrix(table, member):
    if table is None:
        return None
    return table[member]


def attend(hidden, qkv_words, qkv_regions, out_words, out_regions, allowed):
    projected = [
        contract_in(hidden, qkv_words[member], region_matrix(qkv_regions, member)).astype(
            jnp.bfloat16
        )
        for member in range(3)
    ]
    query_b, key_b, value_b = projected
    scores = masked_scores(head_split(query_b), head_split(key_b), allowed)
    top_score = jnp.max(scores, axis=-1, keepdims=True)
    exponent = jnp.exp(scores - top_score)
    denominator = jnp.sum(exponent, axis=-1, keepdims=True)
    attention_probs = exponent / denominator
    log_total = top_score + jnp.log(denominator)
    context_b = (
        jnp.einsum(
            "rhqk,rkhd->rqhd",
            attention_probs.astype(jnp.bfloat16),
            head_split(value_b),
            preferred_element_type=jnp.float32,
        )
        .reshape(query_b.shape)
        .astype(jnp.bfloat16)
    )
    partial_out = contract_in(context_b, out_words, out_regions)
    return (partial_out, (query_b, key_b, value_b, log_total, context_b))


def attend_back(
    hidden, grad_b, kept_values, qkv_words, qkv_regions, out_words, out_regions, allowed
):
    query_b, key_b, value_b, log_total, context_b = kept_values
    by_modality = qkv_regions is not None
    out_weight_grad = weight_grad(context_b, grad_b, by_modality)
    context_grad = head_split(contract_back(grad_b, out_words, out_regions).astype(jnp.bfloat16))
    query_heads = head_split(query_b)
    key_heads = head_split(key_b)
    attention_probs = jnp.exp(masked_scores(query_heads, key_heads, allowed) - log_total)
    probs_grad = jnp.einsum(
        "rqhd,rkhd->rhqk", context_grad, head_split(value_b), preferred_element_type=jnp.float32
    )
    score_grad = (
        attention_probs
        * (probs_grad - jnp.sum(attention_probs * probs_grad, axis=-1, keepdims=True))
    ).astype(jnp.bfloat16)
    scaling = HEAD_DIM ** (-0.5)
    query_grad = (
        (
            jnp.einsum("rhqk,rkhd->rqhd", score_grad, key_heads, preferred_element_type=jnp.float32)
            * scaling
        )
        .reshape(query_b.shape)
        .astype(jnp.bfloat16)
    )
    key_grad = (
        (
            jnp.einsum(
                "rhqk,rqhd->rkhd", score_grad, query_heads, preferred_element_type=jnp.float32
            )
            * scaling
        )
        .reshape(key_b.shape)
        .astype(jnp.bfloat16)
    )
    value_grad = (
        jnp.einsum(
            "rhqk,rqhd->rkhd",
            attention_probs.astype(jnp.bfloat16),
            context_grad,
            preferred_element_type=jnp.float32,
        )
        .reshape(value_b.shape)
        .astype(jnp.bfloat16)
    )
    member_grads = [query_grad, key_grad, value_grad]
    qkv_grad = jnp.stack(
        [weight_grad(hidden, member_grads[member], by_modality) for member in range(3)],
        axis=1 if by_modality else 0,
    )
    hidden_grad = contract_back(query_grad, qkv_words[0], region_matrix(qkv_regions, 0))
    hidden_grad = hidden_grad + contract_back(key_grad, qkv_words[1], region_matrix(qkv_regions, 1))
    hidden_grad = hidden_grad + contract_back(
        value_grad, qkv_words[2], region_matrix(qkv_regions, 2)
    )
    return (hidden_grad, qkv_grad, out_weight_grad)


def norm_forward(summed, gain_rows, shift_rows):
    center = summed - jnp.mean(summed, axis=-1, keepdims=True)
    inverse = lax.rsqrt(jnp.mean(center * center, axis=-1, keepdims=True) + NORM_EPSILON)
    normed = center * inverse
    return (normed * gain_rows + shift_rows, normed, inverse)


def norm_backward(upstream, normed, inverse, gain_rows):
    scaled = upstream * gain_rows
    return inverse * (
        scaled
        - jnp.mean(scaled, axis=-1, keepdims=True)
        - normed * jnp.mean(scaled * normed, axis=-1, keepdims=True)
    )


def exact_gelu(values):
    return jax.nn.gelu(values, approximate=False)


def spread(piece_b):
    return lax.all_gather(piece_b, "tensor", axis=1, tiled=True)


def collect(partial_grad):
    return lax.psum_scatter(
        partial_grad.astype(jnp.bfloat16), "tensor", scatter_dimension=1, tiled=True
    ).astype(jnp.float32)


def widen(piece_b):
    return spread(piece_b)


def finish(partial_out):
    return lax.psum_scatter(
        partial_out.astype(jnp.bfloat16), "tensor", scatter_dimension=1, tiled=True
    ).astype(jnp.float32)


def back_sum(partial_grad):
    return collect(partial_grad)


def body(
    layer_input,
    word_segments,
    image_order,
    cross_qkv,
    cross_out,
    self_qkv,
    self_out,
    ffn_up,
    ffn_down,
    norm_gains,
    norm_biases,
    out_grad,
):
    row_count = layer_input.shape[0]
    share_len = layer_input.shape[1]
    slot_count = share_len * lax.axis_size("tensor")
    tensor_place = lax.axis_index("tensor")
    groups = jnp.concatenate(
        [
            word_segments,
            jnp.repeat(image_order, BOXES, axis=1),
            jnp.full((row_count, PADS), CAPTIONS, jnp.int32),
        ],
        axis=1,
    )
    slot_ids = jnp.arange(slot_count)
    slot_kind = jnp.where(slot_ids < WORDS, 0, jnp.where(slot_ids < WORDS + REGIONS, 1, 2))
    same_group = groups[:, :, None] == groups[:, None, :]
    differ = slot_kind[:, None] != slot_kind[None, :]
    cross_ok = same_group & (differ | (slot_kind[:, None] == 2))[None]
    self_ok = same_group & jnp.logical_not(differ)[None]
    stream_ids = tensor_place * share_len + jnp.arange(share_len)
    stream_word = (stream_ids < WORDS)[:, None]
    own_rows = (stream_ids // share_len == tensor_place).astype(jnp.float32)[:, None]
    word_weight = stream_word.astype(jnp.float32) * own_rows
    other_weight = own_rows - word_weight

    def pick(table, first_norm, second_norm):
        return jnp.where(stream_word, table[first_norm], table[second_norm])

    def norm_terms(upstream, normed, first_norm, second_norm, gain_grad, bias_grad):
        gain_terms = upstream * normed
        gain_grad = gain_grad.at[first_norm].add(jnp.sum(gain_terms * word_weight, axis=(0, 1)))
        gain_grad = gain_grad.at[second_norm].add(jnp.sum(gain_terms * other_weight, axis=(0, 1)))
        bias_grad = bias_grad.at[first_norm].add(jnp.sum(upstream * word_weight, axis=(0, 1)))
        bias_grad = bias_grad.at[second_norm].add(jnp.sum(upstream * other_weight, axis=(0, 1)))
        return (gain_grad, bias_grad)

    input_full = spread(layer_input)
    stream = layer_input.astype(jnp.float32)
    cross_part, cross_kept = attend(input_full, cross_qkv, None, cross_out, None, cross_ok)
    section_one, normed_one, inverse_one = norm_forward(
        stream + finish(cross_part), norm_gains[0], norm_biases[0]
    )
    one_full = widen(section_one.astype(jnp.bfloat16))
    self_part, self_kept = attend(
        one_full, self_qkv[0], self_qkv[1], self_out[0], self_out[1], self_ok
    )
    gains_two = pick(norm_gains, 1, 2)
    section_two, normed_two, inverse_two = norm_forward(
        section_one + finish(self_part), gains_two, pick(norm_biases, 1, 2)
    )
    two_full = widen(section_two.astype(jnp.bfloat16))
    upward = contract_in(two_full, ffn_up[0], ffn_up[1])
    active, gelu_pull = jax.vjp(exact_gelu, upward)
    active_b = active.astype(jnp.bfloat16)
    ffn_part = contract_in(active_b, ffn_down[0], ffn_down[1])
    gains_three = pick(norm_gains, 3, 4)
    result, normed_three, inverse_three = norm_forward(
        section_two + finish(ffn_part), gains_three, pick(norm_biases, 3, 4)
    )
    layer_output = result.astype(jnp.bfloat16)
    upstream = out_grad.astype(jnp.float32)
    gain_grad, bias_grad = norm_terms(
        upstream, normed_three, 3, 4, jnp.zeros_like(norm_gains), jnp.zeros_like(norm_biases)
    )
    grad_three = norm_backward(upstream, normed_three, inverse_three, gains_three)
    three_full = widen(grad_three.astype(jnp.bfloat16))
    down_grad = weight_grad(active_b, three_full, True)
    active_grad = contract_back(three_full, ffn_down[0], ffn_down[1])
    upward_grad = gelu_pull(active_grad)[0].astype(jnp.bfloat16)
    up_grad = weight_grad(two_full, upward_grad, True)
    section_two_grad = grad_three + back_sum(contract_back(upward_grad, ffn_up[0], ffn_up[1]))
    gain_grad, bias_grad = norm_terms(section_two_grad, normed_two, 1, 2, gain_grad, bias_grad)
    grad_two = norm_backward(section_two_grad, normed_two, inverse_two, gains_two)
    two_back = widen(grad_two.astype(jnp.bfloat16))
    hidden_two, self_qkv_grad, self_out_grad = attend_back(
        one_full, two_back, self_kept, self_qkv[0], self_qkv[1], self_out[0], self_out[1], self_ok
    )
    section_one_grad = grad_two + back_sum(hidden_two)
    gain_grad, bias_grad = norm_terms(section_one_grad, normed_one, 0, 0, gain_grad, bias_grad)
    grad_one = norm_backward(section_one_grad, normed_one, inverse_one, norm_gains[0])
    one_back = widen(grad_one.astype(jnp.bfloat16))
    hidden_one, cross_qkv_grad, cross_out_grad = attend_back(
        input_full, one_back, cross_kept, cross_qkv, None, cross_out, None, cross_ok
    )
    input_grad = grad_one + collect(hidden_one)
    summed_grads = lax.psum(
        (cross_qkv_grad, cross_out_grad, self_qkv_grad, self_out_grad, up_grad, down_grad), "dp"
    )
    norm_grads = lax.psum((gain_grad, bias_grad), ("dp", "tensor"))
    return (
        layer_output,
        input_grad,
        summed_grads[0],
        summed_grads[1],
        summed_grads[2],
        summed_grads[3],
        summed_grads[4],
        summed_grads[5],
        norm_grads[0],
        norm_grads[1],
    )


def solution(mesh):
    in_specs = (
        P("dp", "tensor", None),
        P("dp", None),
        P("dp", None),
        P(None, None, "tensor"),
        P("tensor", None),
        P(None, None, None, "tensor"),
        P(None, "tensor", None),
        P(None, None, "tensor"),
        P(None, "tensor", None),
        P(),
        P(),
        P("dp", "tensor", None),
    )
    out_specs = (
        P("dp", "tensor", None),
        P("dp", "tensor", None),
        P(None, None, "tensor"),
        P("tensor", None),
        P(None, None, None, "tensor"),
        P(None, "tensor", None),
        P(None, None, "tensor"),
        P(None, "tensor", None),
        P(),
        P(),
    )
    return jax.shard_map(body, mesh=mesh, in_specs=in_specs, out_specs=out_specs, check_vma=False)
```

profile of v0, /device:TPU:0, one launch (start us, length us, event | category | flops | bytes accessed | tf_op | source)
XLA Modules:
  0.0 1024.6 jit_solution(17787400769139441836)
XLA Ops:
  10.3 2.4 compare_and_fusion.1
  12.7 50.1 %all-gather.7.cloned.1.call-done = bf16[2,768,768]{2,1,0:T(8,128)(2,1)} async-done(((bf16[2,192,768]{2,1,0:T(8,128)(2,1)}), bf16[2,768,768]{2,1,0:T(8,128)(2,1)}) %all-gather.7.cloned.1.call-update) | async-done | bytes 2359312 | tf_op jit(solution)/shard_map/all_gather | solution.py:198
  62.8 2.7 convolution_convert_fusion.9
  66.5 6.6 fusion.197
  73.1 6.9 fusion
  80.9 6.7 fusion.55
  88.5 2.2 convolution_convert_fusion
  91.6 46.3 %reduce-scatter.7.cloned.1.call-done = bf16[2,192,768]{2,1,0:T(8,128)(2,1)} async-done(((bf16[2,768,768]{2,1,0:T(8,128)(2,1)}), bf16[2,192,768]{2,1,0:T(8,128)(2,1)}) %reduce-scatter.7.cloned.1.call-update) | async-done | bytes 589840 | tf_op jit(solution)/shard_map/reduce_scatter | solution.py:212
  142.0 1.5 fusion.195
  143.6 48.3 %all-gather.9.cloned.1.call-done = bf16[2,768,768]{2,1,0:T(8,128)(2,1)} async-done(((bf16[2,192,768]{2,1,0:T(8,128)(2,1)}), bf16[2,768,768]{2,1,0:T(8,128)(2,1)}) %all-gather.9.cloned.1.call-update) | async-done | bytes 2359312 | tf_op jit(solution)/shard_map/all_gather | solution.py:198
  191.9 2.2 fusion.65
  195.9 6.5 fusion.198
  202.5 6.9 fusion.1
  210.5 6.6 fusion.54
  218.2 1.6 pad_maximum_fusion.5
  221.8 45.0 %reduce-scatter.9.cloned.1.call-done = bf16[2,192,768]{2,1,0:T(8,128)(2,1)} async-done(((bf16[2,768,768]{2,1,0:T(8,128)(2,1)}), bf16[2,192,768]{2,1,0:T(8,128)(2,1)}) %reduce-scatter.9.cloned.1.call-update) | async-done | bytes 589840 | tf_op jit(solution)/shard_map/reduce_scatter | solution.py:212
  266.8 1.6 fusion.194
  270.3 49.7 %all-gather.11.cloned.1.call-done = bf16[2,768,768]{2,1,0:T(8,128)(2,1)} async-done(((bf16[2,192,768]{2,1,0:T(8,128)(2,1)}), bf16[2,768,768]{2,1,0:T(8,128)(2,1)}) %all-gather.11.cloned.1.call-update) | async-done | bytes 2359312 | tf_op jit(solution)/shard_map/all_gather | solution.py:198
  320.0 3.3 fusion.42
  323.3 2.5 fusion.84
  325.8 11.2 %multiply_convert_fusion.2 = (bf16[2,768,768]{2,1,0:T(8,128)(2,1)S(1)}, f32[2,768,768]{2,1,0:T(8,128)}) fusion(f32[2,512,768]{2,1,0:T(8,128)S(1)} %fusion.42, f32[2,256,768]{2,1,0:T(8,128)S(1)} %fusion.84), kind=kLoop, calls=%fused_computation.35 | loop fusion | flops 77856768 | bytes 11796480 | tf_op jit(solution)/shard_map/convert_element_type | solution.py:287
  339.3 1.6 pad_maximum_fusion.6
  341.0 46.9 %reduce-scatter.11.cloned.1.call-done = bf16[2,192,768]{2,1,0:T(8,128)(2,1)} async-done(((bf16[2,768,768]{2,1,0:T(8,128)(2,1)}), bf16[2,192,768]{2,1,0:T(8,128)(2,1)}) %reduce-scatter.11.cloned.1.call-update) | async-done | bytes 589840 | tf_op jit(solution)/shard_map/reduce_scatter | solution.py:212
  387.9 1.9 fusion.192
  392.9 50.1 %all-gather.13.cloned.1.call-done = bf16[2,768,768]{2,1,0:T(8,128)(2,1)} async-done(((bf16[2,192,768]{2,1,0:T(8,128)(2,1)}), bf16[2,768,768]{2,1,0:T(8,128)(2,1)}) %all-gather.13.cloned.1.call-update) | async-done | bytes 2359312 | tf_op jit(solution)/shard_map/all_gather | solution.py:198
  443.0 3.3 fusion.37
  446.3 2.1 fusion.78
  448.4 3.8 add_convert_fusion.1
  454.5 1.6 pad_maximum_fusion.7
  456.3 46.8 %reduce-scatter.13.cloned.1.call-done = bf16[2,192,768]{2,1,0:T(8,128)(2,1)} async-done(((bf16[2,768,768]{2,1,0:T(8,128)(2,1)}), bf16[2,192,768]{2,1,0:T(8,128)(2,1)}) %reduce-scatter.13.cloned.1.call-update) | async-done | bytes 589840 | tf_op jit(solution)/shard_map/reduce_scatter | solution.py:202
  503.1 4.5 multiply_reduce_fusion.8
  510.8 49.2 %all-gather.15.cloned.1.call-done = bf16[2,768,768]{2,1,0:T(8,128)(2,1)} async-done(((bf16[2,192,768]{2,1,0:T(8,128)(2,1)}), bf16[2,768,768]{2,1,0:T(8,128)(2,1)}) %all-gather.15.cloned.1.call-update) | async-done | bytes 2359312 | tf_op jit(solution)/shard_map/all_gather | solution.py:198
  560.0 2.1 fusion.68
  562.2 1.7 convolution_convert_fusion.11
  563.9 11.5 %multiply_reduce_fusion.1 = (f32[2,3,768]{2,1,0:T(4,128)S(1)}, f32[2,3,768,768]{2,3,1,0:T(8,128)}) fusion(f32[2,3,768,768]{2,3,1,0:T(8,128)} %get-tuple-element.242, f32[2,3,768]{2,1,0:T(4,128)S(1)} %log_add_fusion.1, bf16[2,512,3,64]{1,3,2,0:T(8,128)(2,1)S(1)} %copy-done.54, bf16[2,256,3,64]{1,3,2,0:T(8,128)(2,1)S(1)} %convolution_convert_fusion.14, ...), kind=kOutput, calls=%fused_computation.4 | convolution fusion | flops 465956352 | bytes 29528064 | tf_op jit(solution)/shard_map/rqhd,rkhd->rhqk/dot_general | solution.py:128
  575.5 6.9 multiply_convert_fusion.1
  585.0 3.2 fusion.45
  588.2 2.3 fusion.125
  590.5 1.6 fusion.142
  592.1 2.3 fusion.48
  594.4 1.8 fusion.122
  597.7 2.0 fusion.14
  600.0 46.8 %reduce-scatter.15.cloned.1.call-done = bf16[2,192,768]{2,1,0:T(8,128)(2,1)} async-done(((bf16[2,768,768]{2,1,0:T(8,128)(2,1)}), bf16[2,192,768]{2,1,0:T(8,128)(2,1)}) %reduce-scatter.15.cloned.1.call-update) | async-done | bytes 589840 | tf_op jit(solution)/shard_map/reduce_scatter | solution.py:202
  646.8 2.9 multiply_reduce_fusion.6
  652.1 3.7 convolution_bitcast_fusion.3
  655.8 3.6 convolution_bitcast_fusion.1
  659.4 2.9 convolution_bitcast_fusion.2
  662.3 2.8 convolution_bitcast_fusion
  665.1 37.0 %all-gather.17.cloned.1.call-done = bf16[2,768,768]{2,1,0:T(8,128)(2,1)} async-done(((bf16[2,192,768]{2,1,0:T(8,128)(2,1)}), bf16[2,768,768]{2,1,0:T(8,128)(2,1)}) %all-gather.17.cloned.1.call-update) | async-done | bytes 2359312 | tf_op jit(solution)/shard_map/all_gather | solution.py:198
  702.1 2.6 convolution_convert_fusion.7
  704.7 13.0 %multiply_reduce_fusion = (f32[2,3,768]{2,1,0:T(4,128)S(1)}, f32[2,3,768,768]{2,3,1,0:T(8,128)}) fusion(f32[2,3,768,768]{2,3,1,0:T(8,128)} %get-tuple-element.240, f32[2,3,768]{2,1,0:T(4,128)S(1)} %log_add_fusion, bf16[2,768,3,64]{1,3,2,0:T(8,128)(2,1)S(1)} %bitcast.317, bf16[2,768,3,64]{1,3,2,0:T(8,128)(2,1)S(1)} %bitcast.326), kind=kOutput, calls=%fused_computation.1 | convolution fusion | flops 463597056 | bytes 29528064 | tf_op jit(solution)/shard_map/rqhd,rkhd->rhqk/dot_general | solution.py:128
  718.4 6.9 multiply_convert_fusion
  726.7 2.2 fusion.47
  729.0 2.3 fusion.51
  732.9 2.2 add_convert_fusion
  735.5 5.0 pad_maximum_fusion.2
  740.6 2.6 pad_maximum_fusion.3
  750.8 2.0 pad_maximum_fusion.4
  761.4 41.1 %all-reduce.2 = (f32[5,768]{1,0:T(8,128)}, f32[5,768]{1,0:T(8,128)}) all-reduce(f32[5,768]{1,0:T(8,128)S(1)} %scatter-add.49, f32[5,768]{1,0:T(8,128)S(1)} %scatter-add.59), channel_id=1, replica_groups=mesh['dp'=8,'tensor'=4] {'dp','tensor'}, use_global_device_ids=true, to_apply=%region_36.37 | all-reduce | flops 7680 | bytes 61440 | tf_op jit(solution)/shard_map/psum | solution.py:322
  802.4 2.6 convert_add_fusion
  805.0 199.7 %all-reduce.6.cloned.1.call-done = (f32[3,768,192]{1,2,0:T(8,128)}, f32[192,768]{1,0:T(8,128)}, f32[2,3,768,192]{2,3,0,1:T(8,128)}, f32[2,192,768]{2,1,0:T(8,128...) async-done(((f32[3,768,192]{1,2,0:T(8,128)}, f32[192,768]{1,0:T(8,128)}, f32[2,3,768,192]{2,3,0,1:T(8,128)}, f32[2,192,768]{2,1,0:T(8,128)}, f32[2,768,768]{2,1,0:T(8,128)}, ...) | async-done | bytes 16515088 | tf_op jit(solution)/shard_map/psum | solution.py:319
  1004.7 4.3 copy.47
  1012.9 2.2 copy.83
  1015.4 2.2 copy.84
  (343 shorter events, 59.9 us)
Async XLA Ops:
  7.2 81.3 %copy-start = (bf16[192,768]{1,0:T(8,128)(2,1)S(1)}, bf16[192,768]{1,0:T(8,128)(2,1)}, u32[]{:S(2)}) copy-start(bf16[192,768]{1,0:T(8,128)(2,1)} %param.40) | copy-start | bytes 884740
  7.2 55.6 %all-gather.7.cloned.1.call-start = ((), (), s32[]{:S(2)}) async-start(), calls=%async_computation.6 | async-start | bytes 2949120 | tf_op jit(solution)/shard_map/all_gather | solution.py:198
  7.9 129.9 %reduce-scatter.7.cloned.1.call-start = ((), (), s32[]{:S(2)}) async-start(), calls=%async_computation.7 | async-start | bytes 2949120 | tf_op jit(solution)/shard_map/reduce_scatter | solution.py:212
  9.6 53.2 %copy-start.46 = (bf16[3,768,192]{1,2,0:T(8,128)(2,1)S(1)}, bf16[3,768,192]{1,2,0:T(8,128)(2,1)}, u32[]{:S(2)}) copy-start(bf16[3,768,192]{1,2,0:T(8,128)(2,1)} %param.39) | copy-start | bytes 2654212
  65.6 7.5 copy-start.34
  66.5 6.6 copy-start.32
  80.9 6.8 copy-start.51
  88.5 49.3 %copy-start.1 = (bf16[2,192,768]{2,1,0:T(8,128)(2,1)S(1)}, bf16[2,192,768]{2,1,0:T(8,128)(2,1)}, u32[]{:S(2)}) copy-start(bf16[2,192,768]{2,1,0:T(8,128)(2,1)} %param.36) | copy-start | bytes 1769476
  90.8 101.1 %all-gather.9.cloned.1.call-start = ((), (), s32[]{:S(2)}) async-start(), calls=%async_computation.8 | async-start | bytes 2949120 | tf_op jit(solution)/shard_map/all_gather | solution.py:198
  141.8 125.1 %reduce-scatter.9.cloned.1.call-start = ((), (), s32[]{:S(2)}) async-start(), calls=%async_computation.9 | async-start | bytes 2949120 | tf_op jit(solution)/shard_map/reduce_scatter | solution.py:212
  194.5 7.9 copy-start.64
  195.2 7.2 copy-start.55
  195.7 6.8 copy-start.62
  209.4 7.7 copy-start.66
  210.1 7.1 copy-start.53
  210.5 6.7 copy-start.36
  219.8 100.2 %all-gather.11.cloned.1.call-start = ((), (), s32[]{:S(2)}) async-start(), calls=%async_computation.10 | async-start | bytes 2949120 | tf_op jit(solution)/shard_map/all_gather | solution.py:198
  221.8 48.0 %copy-start.4 = (f32[192,768]{1,0:T(8,128)}, f32[192,768]{1,0:T(8,128)S(1)}, u32[]{:S(2)}) copy-start(f32[192,768]{1,0:T(8,128)S(1)} %get-tuple-element.238) | copy-start | bytes 1769476
  268.7 238.9 %copy-start.68 = (f32[2,192]{1,0:T(2,128)}, f32[2,192]{1,0:T(2,128)S(1)}, u32[]{:S(2)}) copy-start(f32[2,192]{1,0:T(2,128)S(1)} %add_rsqrt_fusion.1) | copy-start | bytes 4612
  269.9 118.0 %reduce-scatter.11.cloned.1.call-start = ((), (), s32[]{:S(2)}) async-start(), calls=%async_computation.11 | async-start | bytes 2949120 | tf_op jit(solution)/shard_map/reduce_scatter | solution.py:212
  323.3 13.8 %copy-start.7 = (f32[2,512,768]{2,1,0:T(8,128)}, f32[2,512,768]{2,1,0:T(8,128)S(1)}, u32[]{:S(2)}) copy-start(f32[2,512,768]{2,1,0:T(8,128)S(1)} %fusion.42) | copy-start | bytes 9437188
  325.8 11.2 %copy-start.17 = (f32[2,256,768]{2,1,0:T(8,128)}, f32[2,256,768]{2,1,0:T(8,128)S(1)}, u32[]{:S(2)}) copy-start(f32[2,256,768]{2,1,0:T(8,128)S(1)} %fusion.84) | copy-start | bytes 4718596
  325.8 11.2 %copy-start.90 = (bf16[2,768,768]{2,1,0:T(8,128)(2,1)S(1)}, bf16[2,768,768]{2,1,0:T(8,128)(2,1)}, u32[]{:S(2)}) copy-start(bf16[2,768,768]{2,1,0:T(8,128)(2,1)} %param.44) | copy-start | bytes 7077892
  340.9 102.1 %all-gather.13.cloned.1.call-start = ((), (), s32[]{:S(2)}) async-start(), calls=%async_computation.12 | async-start | bytes 2949120 | tf_op jit(solution)/shard_map/all_gather | solution.py:198
  341.0 49.2 %copy-start.76 = (f32[192]{0:T(256)}, f32[192]{0:T(256)S(1)}, u32[]{:S(2)}) copy-start(f32[192]{0:T(256)S(1)} %get-tuple-element.248) | copy-start | bytes 2308
  341.0 162.1 %copy-start.74 = (f32[192]{0:T(256)}, f32[192]{0:T(256)S(1)}, u32[]{:S(2)}) copy-start(f32[192]{0:T(256)S(1)} %get-tuple-element.247) | copy-start | bytes 2308
  392.8 110.3 %reduce-scatter.13.cloned.1.call-start = ((), (), s32[]{:S(2)}) async-start(), calls=%async_computation.13 | async-start | bytes 2949120 | tf_op jit(solution)/shard_map/reduce_scatter | solution.py:202
  443.0 5.4 copy-start.18
  448.4 3.8 copy-start.93
  456.1 103.9 %all-gather.15.cloned.1.call-start = ((), (), s32[]{:S(2)}) async-start(), calls=%async_computation.14 | async-start | bytes 2949120 | tf_op jit(solution)/shard_map/all_gather | solution.py:198
  503.1 5.6 copy-start.5
  509.9 136.9 %reduce-scatter.15.cloned.1.call-start = ((), (), s32[]{:S(2)}) async-start(), calls=%async_computation.15 | async-start | bytes 2949120 | tf_op jit(solution)/shard_map/reduce_scatter | solution.py:202
  510.8 53.1 %copy-start.54 = (bf16[2,512,3,64]{1,3,2,0:T(8,128)(2,1)S(1)}, bf16[2,512,3,64]{1,3,2,0:T(8,128)(2,1)}, u32[]{:S(2)}) copy-start(bf16[2,512,3,64]{1,3,2,0:T(8,128)(2,1)} %copy-done.53) | copy-start | bytes 1179652
  562.2 13.2 %slice-start.4 = ((s8[14155776]{0:T(1024)(128)(4,1)}), s8[4194304]{0:T(1024)(128)(4,1)S(1)}, s32[]{:S(2)}) async-start(s8[14155776]{0:T(1024)(128)(4,1)} %bitcast.291), calls=%async_computation.23 | async-start | bytes 8388608
  563.9 11.5 %slice-start.5 = ((s8[14155776]{0:T(1024)(128)(4,1)}), s8[4194304]{0:T(1024)(128)(4,1)S(1)}, s32[]{:S(2)}) async-start(s8[14155776]{0:T(1024)(128)(4,1)} %bitcast.291), calls=%async_computation.24 | async-start | bytes 8388608
  563.9 11.5 %slice-start.6 = ((s8[14155776]{0:T(1024)(128)(4,1)}), s8[4194304]{0:T(1024)(128)(4,1)S(1)}, s32[]{:S(2)}) async-start(s8[14155776]{0:T(1024)(128)(4,1)} %bitcast.291), calls=%async_computation.25 | async-start | bytes 8388608
  563.9 11.5 %slice-start.7 = ((s8[14155776]{0:T(1024)(128)(4,1)}), s8[1572864]{0:T(1024)(128)(4,1)S(1)}, s32[]{:S(2)}) async-start(s8[14155776]{0:T(1024)(128)(4,1)} %bitcast.291), calls=%async_computation.26 | async-start | bytes 3145728
  575.5 7.0 copy-start.57
  575.5 7.0 copy-start.65
  588.2 3.9 copy-start.28
  599.7 47.1 %copy-start.3 = (bf16[2,192,768]{2,1,0:T(8,128)(2,1)S(1)}, bf16[2,192,768]{2,1,0:T(8,128)(2,1)}, u32[]{:S(2)}) copy-start(bf16[2,192,768]{2,1,0:T(8,128)(2,1)} %reduce-scatter.7.cloned.1.call-done) | copy-start | bytes 1769476
  599.7 47.1 %copy-start.6 = (f32[192,768]{1,0:T(8,128)S(1)}, f32[192,768]{1,0:T(8,128)}, u32[]{:S(2)}) copy-start(f32[192,768]{1,0:T(8,128)} %copy-done.4) | copy-start | bytes 1769476
  599.7 47.1 %copy-start.69 = (f32[2,192]{1,0:T(2,128)S(1)}, f32[2,192]{1,0:T(2,128)}, u32[]{:S(2)}) copy-start(f32[2,192]{1,0:T(2,128)} %copy-done.68) | copy-start | bytes 4612
  599.7 47.1 %copy-start.71 = (f32[2,192]{1,0:T(2,128)S(1)}, f32[2,192]{1,0:T(2,128)}, u32[]{:S(2)}) copy-start(f32[2,192]{1,0:T(2,128)} %copy-done.70) | copy-start | bytes 4612
  599.7 47.1 %copy-start.73 = (f32[2,192]{1,0:T(2,128)S(1)}, f32[2,192]{1,0:T(2,128)}, u32[]{:S(2)}) copy-start(f32[2,192]{1,0:T(2,128)} %copy-done.72) | copy-start | bytes 4612
  599.7 47.1 %copy-start.75 = (f32[192]{0:T(256)S(1)}, f32[192]{0:T(256)}, u32[]{:S(2)}) copy-start(f32[192]{0:T(256)} %copy-done.74) | copy-start | bytes 2308
  599.7 47.1 %copy-start.77 = (f32[192]{0:T(256)S(1)}, f32[192]{0:T(256)}, u32[]{:S(2)}) copy-start(f32[192]{0:T(256)} %copy-done.76) | copy-start | bytes 2308
  599.7 102.4 %all-gather.17.cloned.1.call-start = ((), (), s32[]{:S(2)}) async-start(), calls=%async_computation.16 | async-start | bytes 2949120 | tf_op jit(solution)/shard_map/all_gather | solution.py:198
  652.0 150.5 %reduce-scatter.17.cloned.1.call-start = ((), (), s32[]{:S(2)}) async-start(), calls=%async_computation.17 | async-start | bytes 2949120 | tf_op jit(solution)/shard_map/reduce_scatter | solution.py:202
  652.0 3.8 copy-start.23
  652.0 7.3 copy-start.60
  665.1 39.6 %copy-start.52 = (bf16[2,768,192]{1,2,0:T(8,128)(2,1)S(1)}, bf16[2,768,192]{1,2,0:T(8,128)(2,1)}, u32[]{:S(2)}) copy-start(bf16[2,768,192]{1,2,0:T(8,128)(2,1)} %copy-done.51) | copy-start | bytes 1769476
  704.7 13.0 %slice-start = ((s8[14155776]{0:T(1024)(128)(4,1)}), s8[4194304]{0:T(1024)(128)(4,1)S(1)}, s32[]{:S(2)}) async-start(s8[14155776]{0:T(1024)(128)(4,1)} %bitcast.289), calls=%async_computation.19 | async-start | bytes 8388608
  704.7 13.0 %slice-start.1 = ((s8[14155776]{0:T(1024)(128)(4,1)}), s8[4194304]{0:T(1024)(128)(4,1)S(1)}, s32[]{:S(2)}) async-start(s8[14155776]{0:T(1024)(128)(4,1)} %bitcast.289), calls=%async_computation.20 | async-start | bytes 8388608
  704.7 13.0 %slice-start.2 = ((s8[14155776]{0:T(1024)(128)(4,1)}), s8[4194304]{0:T(1024)(128)(4,1)S(1)}, s32[]{:S(2)}) async-start(s8[14155776]{0:T(1024)(128)(4,1)} %bitcast.289), calls=%async_computation.21 | async-start | bytes 8388608
  704.7 13.7 %slice-start.3 = ((s8[14155776]{0:T(1024)(128)(4,1)}), s8[1572864]{0:T(1024)(128)(4,1)S(1)}, s32[]{:S(2)}) async-start(s8[14155776]{0:T(1024)(128)(4,1)} %bitcast.289), calls=%async_computation.22 | async-start | bytes 3145728
  718.4 7.0 copy-start.33
  735.2 269.5 %all-reduce.6.cloned.1.call-start = ((), (), s32[]{:S(2)}) async-start(), calls=%async_computation.18 | async-start | bytes 33030144 | tf_op jit(solution)/shard_map/psum | solution.py:319
  735.5 5.0 copy-start.13
  735.5 5.0 copy-start.40
  759.6 42.8 %copy-start.11 = (f32[2,192,768]{2,1,0:T(8,128)S(1)}, f32[2,192,768]{2,1,0:T(8,128)}, u32[]{:S(2)}) copy-start(f32[2,192,768]{2,1,0:T(8,128)} %copy-done.10) | copy-start | bytes 3538948
  1004.7 4.4 copy-start.41
  1004.7 6.6 copy-start.42
  1009.1 3.8 copy-start.21
  (56 other events, 105.9 us)
Sparse Core Ops, SparseCore 0:
  9.6 53.1 all-gather.6
  90.9 46.8 reduce-scatter.6
  141.9 49.9 all-gather.8
  219.9 46.8 reduce-scatter.8
  270.0 49.9 all-gather.10
  341.0 46.8 reduce-scatter.10
  393.0 49.9 all-gather.12
  456.2 46.8 reduce-scatter.12
  510.0 49.9 all-gather.14
  599.8 46.8 reduce-scatter.14
  652.1 49.9 all-gather.16
  735.3 46.9 reduce-scatter.16
  787.8 216.8 all-reduce.5
where the time goes:
time: 1030 us; the launch traced here: 1020 us
  waiting for transfers between devices  717 us (70%)
  matrix products  130 us (13%)
  other arithmetic  91.1 us (9%)
  blocking collectives  41.1 us (4%)
  local copies, waits for them, and re-layouts  28.1 us (3%)
  between operations  16 us (2%)
    all_gather x6, waiting for transfers between devices, spread(): return lax.all_gather(piece_b, 'tensor', axis=1, tiled=True)  284 us
    psum x1, waiting for transfers between devices, body(): lax.psum((cross_qkv_grad, cross_out_grad, self_qkv_grad, self_out_grad, u...  200 us
    reduce_scatter x3, waiting for transfers between devices, finish(): lax.psum_scatter(partial_out.astype(jnp.bfloat16), 'tensor', scatter_dime...  138 us
    reduce_scatter x3, waiting for transfers between devices, collect(): lax.psum_scatter(partial_grad.astype(jnp.bfloat16), 'tensor', scatter_dim...  93.5 us
    psum x1, blocking collectives, body(): norm_grads = lax.psum((gain_grad, bias_grad), ('dp', 'tensor'))  41.1 us
    dot_general x2, matrix products, attend_back(): jnp.einsum('rqhd,rkhd->rhqk', context_grad, head_split(value_b), preferre...  24.4 us
    unnamed x220, local copies, waits for them, and re-layouts  23.2 us
  transfers between devices with their start and end apart: 13, of which 12 were waited for; matrix products, arithmetic and copies ran while one was open for 4% of the time, Pallas kernels for 0%

commit v1 on v0

--- a/solution.py
+++ b/solution.py
@@ -316,9 +316,23 @@
         input_full, one_back, cross_kept, cross_qkv, None, cross_out, None, cross_ok
     )
     input_grad = grad_one + collect(hidden_one)
-    summed_grads = lax.psum(
-        (cross_qkv_grad, cross_out_grad, self_qkv_grad, self_out_grad, up_grad, down_grad), "dp"
-    )
+    summed_grads = [
+        total.astype(jnp.float32)
+        for total in lax.psum(
+            [
+                grad.astype(jnp.bfloat16)
+                for grad in (
+                    cross_qkv_grad,
+                    cross_out_grad,
+                    self_qkv_grad,
+                    self_out_grad,
+                    up_grad,
+                    down_grad,
+                )
+            ],
+            "dp",
+        )
+    ]
     norm_grads = lax.psum((gain_grad, bias_grad), ("dp", "tensor"))
     return (
         layer_output,

time: 1030 us -> 932 us (0.905)
  waiting for transfers between devices: 717 us -> 624 us
    psum x1, waiting for transfers between devices: 200 us -> 79.2 us  [body(): lax.psum([grad.astype(jnp.bfloat16) for grad in (cross_qkv_grad, cross_ou...]
    reduce_scatter x3, waiting for transfers between devices: 93.5 us -> 130 us  [collect(): lax.psum_scatter(partial_grad.astype(jnp.bfloat16), 'tensor', scatter_dim...]
    convert_element_type x0 -> x5, other arithmetic: none -> 10.5 us  [body(): total.astype(jnp.float32)]
    dot_general x2, matrix products: 4.62 us -> 14.9 us  [attend_back(): jnp.einsum('rhqk,rqhd->rkhd', attention_probs.astype(jnp.bfloat16), conte...]
    unnamed x220 -> x215, local copies, waits for them, and re-layouts: 23.2 us -> 15.3 us
  transfers between devices with their start and end apart: 13 -> 13, of which waited for: 12 -> 13; matrix products, arithmetic and copies ran while one was open for 4% -> 5% of each run, Pallas kernels for 0% -> 0%
where the time goes in v1:
time: 932 us; the launch traced here: 923 us
  waiting for transfers between devices  624 us (67%)
  matrix products  124 us (13%)
  other arithmetic  96.2 us (10%)
  blocking collectives  40.8 us (4%)
  local copies, waits for them, and re-layouts  20.7 us (2%)
  between operations  16 us (2%)
    all_gather x6, waiting for transfers between devices, spread(): return lax.all_gather(piece_b, 'tensor', axis=1, tiled=True)  275 us
    reduce_scatter x3, waiting for transfers between devices, finish(): lax.psum_scatter(partial_out.astype(jnp.bfloat16), 'tensor', scatter_dime...  138 us
    reduce_scatter x3, waiting for transfers between devices, collect(): lax.psum_scatter(partial_grad.astype(jnp.bfloat16), 'tensor', scatter_dim...  130 us
    psum x1, waiting for transfers between devices, body(): lax.psum([grad.astype(jnp.bfloat16) for grad in (cross_qkv_grad, cross_ou...  79.2 us
    psum x1, blocking collectives, body(): norm_grads = lax.psum((gain_grad, bias_grad), ('dp', 'tensor'))  40.8 us
  transfers between devices with their start and end apart: 13, of which 13 were waited for; matrix products, arithmetic and copies ran while one was open for 5% of the time, Pallas kernels for 0%

profile of v1, /device:TPU:0, one launch (start us, length us, event | category | flops | bytes accessed | tf_op | source)
XLA Modules:
  0.0 923.2 jit_solution(17433531163479221925)
XLA Ops:
  10.3 2.4 compare_and_fusion.1
  12.7 50.1 %all-gather.7.cloned.1.call-done = bf16[2,768,768]{2,1,0:T(8,128)(2,1)} async-done(((bf16[2,192,768]{2,1,0:T(8,128)(2,1)}), bf16[2,768,768]{2,1,0:T(8,128)(2,1)}) %all-gather.7.cloned.1.call-update) | async-done | bytes 2359312 | tf_op jit(solution)/shard_map/all_gather | solution.py:198
  62.8 2.7 convolution_convert_fusion.8
  66.5 6.6 fusion.228
  73.1 6.9 fusion
  80.9 6.7 fusion.59
  88.5 2.2 convolution_convert_fusion
  91.5 46.3 %reduce-scatter.7.cloned.1.call-done = bf16[2,192,768]{2,1,0:T(8,128)(2,1)} async-done(((bf16[2,768,768]{2,1,0:T(8,128)(2,1)}), bf16[2,192,768]{2,1,0:T(8,128)(2,1)}) %reduce-scatter.7.cloned.1.call-update) | async-done | bytes 589840 | tf_op jit(solution)/shard_map/reduce_scatter | solution.py:212
  143.1 48.7 %all-gather.9.cloned.1.call-done = bf16[2,768,768]{2,1,0:T(8,128)(2,1)} async-done(((bf16[2,192,768]{2,1,0:T(8,128)(2,1)}), bf16[2,768,768]{2,1,0:T(8,128)(2,1)}) %all-gather.9.cloned.1.call-update) | async-done | bytes 2359312 | tf_op jit(solution)/shard_map/all_gather | solution.py:198
  191.8 1.8 convolution_convert_fusion.12
  193.6 1.7 convolution_convert_fusion.13
  196.8 6.5 fusion.229
  203.3 6.9 fusion.1
  211.3 6.6 fusion.58
  219.1 1.6 pad_maximum_fusion.2
  222.9 44.8 %reduce-scatter.9.cloned.1.call-done = bf16[2,192,768]{2,1,0:T(8,128)(2,1)} async-done(((bf16[2,768,768]{2,1,0:T(8,128)(2,1)}), bf16[2,192,768]{2,1,0:T(8,128)(2,1)}) %reduce-scatter.9.cloned.1.call-update) | async-done | bytes 589840 | tf_op jit(solution)/shard_map/reduce_scatter | solution.py:212
  267.7 1.7 fusion.225
  271.2 49.7 %all-gather.11.cloned.1.call-done = bf16[2,768,768]{2,1,0:T(8,128)(2,1)} async-done(((bf16[2,192,768]{2,1,0:T(8,128)(2,1)}), bf16[2,768,768]{2,1,0:T(8,128)(2,1)}) %all-gather.11.cloned.1.call-update) | async-done | bytes 2359312 | tf_op jit(solution)/shard_map/all_gather | solution.py:198
  320.9 2.4 fusion.102
  323.4 3.4 fusion.46
  326.8 11.2 %multiply_convert_fusion.2 = (bf16[2,768,768]{2,1,0:T(8,128)(2,1)S(1)}, f32[2,768,768]{2,1,0:T(8,128)}) fusion(f32[2,512,768]{2,1,0:T(8,128)S(1)} %fusion.46, f32[2,256,768]{2,1,0:T(8,128)S(1)} %fusion.102), kind=kLoop, calls=%fused_computation.33 | loop fusion | flops 77856768 | bytes 11796480 | tf_op jit(solution)/shard_map/convert_element_type | solution.py:287
  340.8 1.6 pad_maximum_fusion.3
  342.5 46.9 %reduce-scatter.11.cloned.1.call-done = bf16[2,192,768]{2,1,0:T(8,128)(2,1)} async-done(((bf16[2,768,768]{2,1,0:T(8,128)(2,1)}), bf16[2,192,768]{2,1,0:T(8,128)(2,1)}) %reduce-scatter.11.cloned.1.call-update) | async-done | bytes 589840 | tf_op jit(solution)/shard_map/reduce_scatter | solution.py:212
  389.4 1.9 fusion.223
  394.4 50.1 %all-gather.13.cloned.1.call-done = bf16[2,768,768]{2,1,0:T(8,128)(2,1)} async-done(((bf16[2,192,768]{2,1,0:T(8,128)(2,1)}), bf16[2,768,768]{2,1,0:T(8,128)(2,1)}) %all-gather.13.cloned.1.call-update) | async-done | bytes 2359312 | tf_op jit(solution)/shard_map/all_gather | solution.py:198
  444.5 2.5 fusion.96
  447.0 3.0 fusion.41
  450.0 3.8 add_convert_fusion.1
  456.1 1.6 pad_maximum_fusion.4
  457.9 46.8 %reduce-scatter.13.cloned.1.call-done = bf16[2,192,768]{2,1,0:T(8,128)(2,1)} async-done(((bf16[2,768,768]{2,1,0:T(8,128)(2,1)}), bf16[2,192,768]{2,1,0:T(8,128)(2,1)}) %reduce-scatter.13.cloned.1.call-update) | async-done | bytes 589840 | tf_op jit(solution)/shard_map/reduce_scatter | solution.py:202
  504.7 4.5 multiply_reduce_fusion.8
  511.5 1.9 fusion.227
  513.4 48.1 %all-gather.15.cloned.1.call-done = bf16[2,768,768]{2,1,0:T(8,128)(2,1)} async-done(((bf16[2,192,768]{2,1,0:T(8,128)(2,1)}), bf16[2,768,768]{2,1,0:T(8,128)(2,1)}) %all-gather.15.cloned.1.call-update) | async-done | bytes 2359312 | tf_op jit(solution)/shard_map/all_gather | solution.py:198
  561.6 1.6 convolution_convert_fusion.11
  563.2 2.3 fusion.72
  565.5 7.5 fusion.52
  573.0 1.6 fusion.170
  575.5 6.3 multiply_reduce_fusion.1
  581.8 6.9 multiply_convert_fusion.1
  588.7 2.2 fusion.49
  595.2 1.9 fusion.14
  597.9 46.3 %reduce-scatter.15.cloned.1.call-done = bf16[2,192,768]{2,1,0:T(8,128)(2,1)} async-done(((bf16[2,768,768]{2,1,0:T(8,128)(2,1)}), bf16[2,192,768]{2,1,0:T(8,128)(2,1)}) %reduce-scatter.15.cloned.1.call-update) | async-done | bytes 589840 | tf_op jit(solution)/shard_map/reduce_scatter | solution.py:202
  644.2 3.0 multiply_reduce_fusion.6
  649.6 3.3 fusion.34
  652.9 2.2 fusion.33
  655.1 1.6 pad_maximum_fusion.6
  660.9 1.6 pad_maximum_fusion.5
  671.1 28.6 %all-gather.17.cloned.1.call-done = bf16[2,768,768]{2,1,0:T(8,128)(2,1)} async-done(((bf16[2,192,768]{2,1,0:T(8,128)(2,1)}), bf16[2,768,768]{2,1,0:T(8,128)(2,1)}) %all-gather.17.cloned.1.call-update) | async-done | bytes 2359312 | tf_op jit(solution)/shard_map/all_gather | solution.py:198
  699.7 2.6 convolution_convert_fusion.7
  702.3 7.4 fusion.55
  709.8 10.3 %multiply_reduce_fusion = (f32[2,3,768]{2,1,0:T(4,128)S(1)}, f32[2,3,768,768]{2,3,1,0:T(8,128)}) fusion(f32[2,3,768,768]{2,3,1,0:T(8,128)} %get-tuple-element.240, f32[2,3,768]{2,1,0:T(4,128)S(1)} %log_add_fusion, bf16[2,768,3,64]{1,3,2,0:T(8,128)(2,1)S(1)} %bitcast.382, bf16[2,768,3,64]{1,3,2,0:T(8,128)(2,1)S(1)} %bitcast.390), kind=kOutput, calls=%fused_computation.1 | convolution fusion | flops 463597056 | bytes 29528064 | tf_op jit(solution)/shard_map/rqhd,rkhd->rhqk/dot_general | solution.py:128
  720.1 6.9 multiply_convert_fusion
  727.1 2.2 fusion.51
  735.9 1.9 fusion.185
  738.6 2.3 add_convert_fusion
  742.7 40.8 %all-reduce.2 = (f32[5,768]{1,0:T(8,128)}, f32[5,768]{1,0:T(8,128)}) all-reduce(f32[5,768]{1,0:T(8,128)S(1)} %scatter-add.49, f32[5,768]{1,0:T(8,128)S(1)} %scatter-add.59), channel_id=1, replica_groups=mesh['dp'=8,'tensor'=4] {'dp','tensor'}, use_global_device_ids=true, to_apply=%region_36.37 | all-reduce | flops 7680 | bytes 61440 | tf_op jit(solution)/shard_map/psum | solution.py:336
  783.5 79.2 %all-reduce.6.cloned.1.call-done = (bf16[2,3,768,192]{2,3,0,1:T(8,128)(2,1)}, bf16[3,768,192]{1,2,0:T(8,128)(2,1)}, bf16[192,768]{1,0:T(8,128)(2,1)}, bf16[2,192...) async-done(((bf16[2,3,768,192]{2,3,0,1:T(8,128)(2,1)}, bf16[3,768,192]{1,2,0:T(8,128)(2,1)}, bf16[192,768]{1,0:T(8,128)(2,1)}, ...) | async-done | bytes 8257552 | tf_op jit(solution)/shard_map/psum | solution.py:321
  862.8 1.9 convert_element_type.270
  864.7 2.2 convert_element_type.272
  866.9 2.1 copy.47
  871.3 2.5 convert_element_type.273
  874.1 2.5 convert_element_type.274
  876.7 36.9 %reduce-scatter.17.cloned.1.call-done = bf16[2,192,768]{2,1,0:T(8,128)(2,1)} async-done(((bf16[2,768,768]{2,1,0:T(8,128)(2,1)}), bf16[2,192,768]{2,1,0:T(8,128)(2,1)}) %reduce-scatter.17.cloned.1.call-update) | async-done | bytes 589840 | tf_op jit(solution)/shard_map/reduce_scatter | solution.py:202
  913.6 2.6 convert_add_fusion
  (342 shorter events, 62.2 us)
Async XLA Ops:
  7.2 81.3 %copy-start = (bf16[192,768]{1,0:T(8,128)(2,1)S(1)}, bf16[192,768]{1,0:T(8,128)(2,1)}, u32[]{:S(2)}) copy-start(bf16[192,768]{1,0:T(8,128)(2,1)} %param.40) | copy-start | bytes 884740
  7.2 55.6 %all-gather.7.cloned.1.call-start = ((), (), s32[]{:S(2)}) async-start(), calls=%async_computation.6 | async-start | bytes 2949120 | tf_op jit(solution)/shard_map/all_gather | solution.py:198
  7.9 129.9 %reduce-scatter.7.cloned.1.call-start = ((), (), s32[]{:S(2)}) async-start(), calls=%async_computation.7 | async-start | bytes 2949120 | tf_op jit(solution)/shard_map/reduce_scatter | solution.py:212
  9.6 53.2 %copy-start.38 = (bf16[3,768,192]{1,2,0:T(8,128)(2,1)S(1)}, bf16[3,768,192]{1,2,0:T(8,128)(2,1)}, u32[]{:S(2)}) copy-start(bf16[3,768,192]{1,2,0:T(8,128)(2,1)} %param.39) | copy-start | bytes 2654212
  65.6 7.5 copy-start.20
  66.5 6.6 copy-start.24
  73.1 7.9 copy-start.54
  80.0 7.7 copy-start.62
  80.9 6.8 copy-start.45
  88.5 49.3 %copy-start.1 = (bf16[2,192,768]{2,1,0:T(8,128)(2,1)S(1)}, bf16[2,192,768]{2,1,0:T(8,128)(2,1)}, u32[]{:S(2)}) copy-start(bf16[2,192,768]{2,1,0:T(8,128)(2,1)} %param.36) | copy-start | bytes 1769476
  90.8 101.1 %all-gather.9.cloned.1.call-start = ((), (), s32[]{:S(2)}) async-start(), calls=%async_computation.8 | async-start | bytes 2949120 | tf_op jit(solution)/shard_map/all_gather | solution.py:198
  91.5 50.5 %copy-start.13 = (bf16[2,3,768,192]{2,3,1,0:T(8,128)(2,1)S(1)}, bf16[2,3,768,192]{2,3,1,0:T(8,128)(2,1)}, u32[]{:S(2)}) copy-start(bf16[2,3,768,192]{2,3,1,0:T(8,128)(2,1)} %param.41) | copy-start | bytes 5308420
  137.8 2.8 copy-start.3
  141.7 126.0 %reduce-scatter.9.cloned.1.call-start = ((), (), s32[]{:S(2)}) async-start(), calls=%async_computation.9 | async-start | bytes 2949120 | tf_op jit(solution)/shard_map/reduce_scatter | solution.py:212
  143.1 52.2 %copy-start.53 = (bf16[1,1,768,192]{2,3,1,0:T(8,128)(2,1)S(1)}, bf16[1,1,768,192]{2,3,1,0:T(8,128)(2,1)}, u32[]{:S(2)}) copy-start(bf16[1,1,768,192]{2,3,1,0:T(8,128)(2,1)} %get-tuple-element.227) | copy-start | bytes 884740
  191.8 3.5 copy-start.94
  193.6 3.1 copy-start.58
  196.0 7.2 copy-start.49
  196.7 6.5 copy-start.47
  203.2 8.1 copy-start.64
  203.3 7.4 copy-start.51
  210.2 7.8 copy-start.66
  210.6 7.3 copy-start.56
  211.3 6.7 copy-start.28
  220.7 100.2 %all-gather.11.cloned.1.call-start = ((), (), s32[]{:S(2)}) async-start(), calls=%async_computation.10 | async-start | bytes 2949120 | tf_op jit(solution)/shard_map/all_gather | solution.py:198
  270.8 118.6 %reduce-scatter.11.cloned.1.call-start = ((), (), s32[]{:S(2)}) async-start(), calls=%async_computation.11 | async-start | bytes 2949120 | tf_op jit(solution)/shard_map/reduce_scatter | solution.py:212
  323.4 3.4 copy-start.16
  326.8 11.2 %copy-start.7 = (f32[2,512,768]{2,1,0:T(8,128)}, f32[2,512,768]{2,1,0:T(8,128)S(1)}, u32[]{:S(2)}) copy-start(f32[2,512,768]{2,1,0:T(8,128)S(1)} %fusion.46) | copy-start | bytes 9437188
  326.8 11.2 %copy-start.88 = (bf16[2,768,768]{2,1,0:T(8,128)(2,1)S(1)}, bf16[2,768,768]{2,1,0:T(8,128)(2,1)}, u32[]{:S(2)}) copy-start(bf16[2,768,768]{2,1,0:T(8,128)(2,1)} %param.44) | copy-start | bytes 7077892
  342.4 102.1 %all-gather.13.cloned.1.call-start = ((), (), s32[]{:S(2)}) async-start(), calls=%async_computation.12 | async-start | bytes 2949120 | tf_op jit(solution)/shard_map/all_gather | solution.py:198
  342.5 162.2 %copy-start.68 = (f32[192]{0:T(256)}, f32[192]{0:T(256)S(1)}, u32[]{:S(2)}) copy-start(f32[192]{0:T(256)S(1)} %get-tuple-element.248) | copy-start | bytes 2308
  394.4 110.3 %reduce-scatter.13.cloned.1.call-start = ((), (), s32[]{:S(2)}) async-start(), calls=%async_computation.13 | async-start | bytes 2949120 | tf_op jit(solution)/shard_map/reduce_scatter | solution.py:202
  447.0 3.0 copy-start.8
  447.0 3.0 copy-start.17
  450.0 3.8 copy-start.91
  457.7 103.9 %all-gather.15.cloned.1.call-start = ((), (), s32[]{:S(2)}) async-start(), calls=%async_computation.14 | async-start | bytes 2949120 | tf_op jit(solution)/shard_map/all_gather | solution.py:198
  504.7 5.5 copy-start.6
  510.2 3.2 copy-start.65
  510.2 3.2 copy-start.67
  510.2 64.9 %slice-start.4 = ((s8[14155776]{0:T(1024)(128)(4,1)}), s8[1572864]{0:T(1024)(128)(4,1)S(1)}, s32[]{:S(2)}) async-start(s8[14155776]{0:T(1024)(128)(4,1)} %bitcast.357), calls=%async_computation.23 | async-start | bytes 3145728
  511.4 132.8 %reduce-scatter.15.cloned.1.call-start = ((), (), s32[]{:S(2)}) async-start(), calls=%async_computation.15 | async-start | bytes 2949120 | tf_op jit(solution)/shard_map/reduce_scatter | solution.py:202
  563.2 12.0 %slice-start.5 = ((s8[14155776]{0:T(1024)(128)(4,1)}), s8[4194304]{0:T(1024)(128)(4,1)S(1)}, s32[]{:S(2)}) async-start(s8[14155776]{0:T(1024)(128)(4,1)} %bitcast.357), calls=%async_computation.24 | async-start | bytes 8388608
  565.4 7.5 copy-start.14
  565.5 9.7 %slice-start.6 = ((s8[14155776]{0:T(1024)(128)(4,1)}), s8[4194304]{0:T(1024)(128)(4,1)S(1)}, s32[]{:S(2)}) async-start(s8[14155776]{0:T(1024)(128)(4,1)} %bitcast.357), calls=%async_computation.25 | async-start | bytes 8388608
  565.5 9.7 %slice-start.7 = ((s8[14155776]{0:T(1024)(128)(4,1)}), s8[4194304]{0:T(1024)(128)(4,1)S(1)}, s32[]{:S(2)}) async-start(s8[14155776]{0:T(1024)(128)(4,1)} %bitcast.357), calls=%async_computation.26 | async-start | bytes 8388608
  581.8 6.9 copy-start.48
  581.8 6.9 copy-start.61
  591.0 2.8 copy-start.31
  597.2 47.0 %copy-start.2 = (bf16[2,192,768]{2,1,0:T(8,128)(2,1)S(1)}, bf16[2,192,768]{2,1,0:T(8,128)(2,1)}, u32[]{:S(2)}) copy-start(bf16[2,192,768]{2,1,0:T(8,128)(2,1)} %param.36) | copy-start | bytes 1769476
  597.2 47.0 %copy-start.4 = (bf16[2,192,768]{2,1,0:T(8,128)(2,1)S(1)}, bf16[2,192,768]{2,1,0:T(8,128)(2,1)}, u32[]{:S(2)}) copy-start(bf16[2,192,768]{2,1,0:T(8,128)(2,1)} %reduce-scatter.7.cloned.1.call-done) | copy-start | bytes 1769476
  597.2 47.0 %copy-start.69 = (f32[192]{0:T(256)S(1)}, f32[192]{0:T(256)}, u32[]{:S(2)}) copy-start(f32[192]{0:T(256)} %copy-done.68) | copy-start | bytes 2308
  597.2 102.5 %all-gather.17.cloned.1.call-start = ((), (), s32[]{:S(2)}) async-start(), calls=%async_computation.16 | async-start | bytes 2949120 | tf_op jit(solution)/shard_map/all_gather | solution.py:198
  649.5 213.2 %all-reduce.6.cloned.1.call-start = ((), (), s32[]{:S(2)}) async-start(), calls=%async_computation.18 | async-start | bytes 16515072 | tf_op jit(solution)/shard_map/psum | solution.py:321
  655.1 3.5 copy-start.96
  702.2 7.5 copy-start.46
  702.3 17.8 %slice-start = ((s8[14155776]{0:T(1024)(128)(4,1)}), s8[4194304]{0:T(1024)(128)(4,1)S(1)}, s32[]{:S(2)}) async-start(s8[14155776]{0:T(1024)(128)(4,1)} %bitcast.355), calls=%async_computation.19 | async-start | bytes 8388608
  702.3 17.8 %slice-start.1 = ((s8[14155776]{0:T(1024)(128)(4,1)}), s8[4194304]{0:T(1024)(128)(4,1)S(1)}, s32[]{:S(2)}) async-start(s8[14155776]{0:T(1024)(128)(4,1)} %bitcast.355), calls=%async_computation.20 | async-start | bytes 8388608
  709.7 10.3 %slice-start.2 = ((s8[14155776]{0:T(1024)(128)(4,1)}), s8[4194304]{0:T(1024)(128)(4,1)S(1)}, s32[]{:S(2)}) async-start(s8[14155776]{0:T(1024)(128)(4,1)} %bitcast.355), calls=%async_computation.21 | async-start | bytes 8388608
  709.7 10.3 %slice-start.3 = ((s8[14155776]{0:T(1024)(128)(4,1)}), s8[1572864]{0:T(1024)(128)(4,1)S(1)}, s32[]{:S(2)}) async-start(s8[14155776]{0:T(1024)(128)(4,1)} %bitcast.355), calls=%async_computation.22 | async-start | bytes 3145728
  720.1 7.0 copy-start.25
  735.8 177.8 %reduce-scatter.17.cloned.1.call-start = ((), (), s32[]{:S(2)}) async-start(), calls=%async_computation.17 | async-start | bytes 2949120 | tf_op jit(solution)/shard_map/reduce_scatter | solution.py:202
  862.7 4.1 copy-start.36
  871.3 2.9 copy-start.26
  874.1 39.5 %copy-start.10 = (f32[2,192,768]{2,1,0:T(8,128)S(1)}, f32[2,192,768]{2,1,0:T(8,128)}, u32[]{:S(2)}) copy-start(f32[2,192,768]{2,1,0:T(8,128)} %copy-done.9) | copy-start | bytes 3538948
  (56 other events, 84.4 us)
Sparse Core Ops, SparseCore 0:
  9.6 53.1 all-gather.6
  90.9 46.8 reduce-scatter.6
  141.8 49.9 all-gather.8
  220.8 46.8 reduce-scatter.8
  270.9 49.9 all-gather.10
  342.5 46.8 reduce-scatter.10
  394.5 49.9 all-gather.12
  457.8 46.8 reduce-scatter.12
  511.6 49.9 all-gather.14
  597.3 46.8 reduce-scatter.14
  649.6 49.9 all-gather.16
  735.9 126.7 all-reduce.5
  865.2 48.4 reduce-scatter.16
